TPU v7x, 512 devices: a whole 4x8x8 slice. The times are simulated.
512 devices in a mesh: row: 16 (over y, z_lo), col: 32 (over z_hi, x, core).
Axes of the slice: x: 4, y: 8, z: 8 (z_hi: 4, z_lo: 2; z = z_hi * 2 + z_lo), core: 2. Of those that a mesh axis runs over, the one named last changes fastest.
Arguments:
- tiles: bfloat16 [16, 32, 32, 256, 256], P('row', 'col'), may hold values from -6 to 6
- tile_ids: int32 [16, 32, 2, 32], P('row', 'col'), may hold values from 0 to 7, as said below
- tile_count: int32 [16, 32], P('row', 'col'), may hold values from 8 to 32
- query_degree: int32 [32768], P('row'), may hold values from 1 to 32
- product_degree: int32 [65536], P('col'), may hold values from 1 to 32
- panel: float32 [64, 65536], P(None, ('col', 'row')), may hold values from -6 to 6
Outputs:
- basis: float32 [64, 65536], P(None, ('col', 'row'))
Inputs may be any that keep to these rules, and one draw needn't show every extreme that they name: `tile_ids`: on each device the 32 (tile row, tile column) pairs are distinct; tile row is below 8 and tile column below 8.
All inputs are finite; a program needn't handle non-finite values.
Results may differ from a plain program's by a relative error of at most 0.0042.
Values may be sent and summed in bfloat16 or wider, within the bound.
A program may use at most 64 MiB of HBM per device.

v0:
```python
import math
import jax
import jax.numpy as jnp
from jax import lax
from jax.sharding import PartitionSpec as P

ITERS = 2
HIGH = lax.Precision.HIGHEST


def orthonormal(lifted, gram):
    lower = jnp.linalg.cholesky(gram)
    return lax.linalg.triangular_solve(lower, lifted, left_side=True, lower=True)


def shards(tiles, tile_ids, tile_count, query_degree, product_degree, panel):
    tile_set = tiles[0, 0]
    slot_ids = tile_ids[0, 0]
    live_count = tile_count[0, 0]
    slots = tile_set.shape[0]
    side = tile_set.shape[1]
    width = panel.shape[0]
    query_tiles = query_degree.shape[0] // side
    product_tiles = product_degree.shape[0] // side
    live_slot = (jnp.arange(slots, dtype=jnp.int32) < live_count).astype(jnp.float32)
    row_hot = (slot_ids[0][:, None] == jnp.arange(query_tiles, dtype=jnp.int32)[None, :]).astype(
        jnp.float32
    ) * live_slot[:, None]
    col_hot = (slot_ids[1][:, None] == jnp.arange(product_tiles, dtype=jnp.int32)[None, :]).astype(
        jnp.float32
    ) * live_slot[:, None]
    qscale = 1.0 / jnp.sqrt(query_degree.astype(jnp.float32))
    pscale = 1.0 / jnp.sqrt(product_degree.astype(jnp.float32))
    row_at = lax.axis_index("row")
    col_at = lax.axis_index("col")
    share = panel.shape[1]
    my_pscale = lax.dynamic_slice_in_dim(pscale, row_at * share, share)
    root_count = math.sqrt(product_degree.shape[0] * lax.axis_size("col"))
    current = panel
    for iteration in range(ITERS):
        scaled = (current * my_pscale[None, :]).astype(jnp.bfloat16)
        scaled_block = lax.all_gather(scaled, "row", axis=1, tiled=True)
        picked = jnp.take(scaled_block.reshape(width, product_tiles, side), slot_ids[1], axis=1)
        products = jnp.einsum("rkj,kij->kri", picked, tile_set, preferred_element_type=jnp.float32)
        partial_sum = jnp.einsum("kq,kri->rqi", row_hot, products, precision=HIGH).reshape(
            width, query_tiles * side
        )
        query_share = lax.psum_scatter(partial_sum, "col", scatter_dimension=1, tiled=True)
        columns = query_share.shape[1]
        my_qscale = lax.dynamic_slice_in_dim(qscale, col_at * columns, columns)
        rounded = (query_share * my_qscale[None, :]).astype(jnp.bfloat16)
        query_block = lax.all_gather(rounded, "col", axis=1, tiled=True)
        backward_picked = jnp.take(
            query_block.reshape(width, query_tiles, side), slot_ids[0], axis=1
        )
        backward_products = jnp.einsum(
            "rki,kij->krj", backward_picked, tile_set, preferred_element_type=jnp.float32
        )
        lifted = (
            lax.psum_scatter(
                jnp.einsum("kp,krj->rpj", col_hot, backward_products, precision=HIGH).reshape(
                    width, product_tiles * side
                ),
                "row",
                scatter_dimension=1,
                tiled=True,
            )
            * my_pscale[None, :]
        )
        gram = lax.psum(jnp.einsum("ri,si->rs", lifted, lifted, precision=HIGH), ("row", "col"))
        current = orthonormal(lifted, gram)
    return current * root_count


def solution(mesh):
    in_specs = (
        P("row", "col", None, None, None),
        P("row", "col", None, None),
        P("row", "col"),
        P("row"),
        P("col"),
        P(None, ("col", "row")),
    )
    out_specs = P(None, ("col", "row"))
    return jax.shard_map(shards, mesh=mesh, in_specs=in_specs, out_specs=out_specs, check_vma=False)
```

profile of v0, /device:TPU:24, one launch (start us, length us, event | category | flops | bytes accessed | tf_op | source)
XLA Modules:
  0.0 757.7 jit_solution(1532699937566994767)
XLA Ops:
  10.3 32.3 %all_gather.12 = bf16[64,2048]{1,0:T(8,128)(2,1)S(1)} all-gather(bf16[64,128]{1,0:T(8,128)(2,1)S(1)} %multiply_convert_fusion.2), channel_id=1, replica_groups=mesh['row'=16,'col'=32] {'row'}, dimensions={1}, use_global_device_ids=true | all-gather | bytes 278528 | tf_op jit(solution)/shard_map/all_gather | solution.py:42
  43.2 3.6 fusion.6
  46.8 2.4 fusion.16
  49.1 1.4 copy.55
  51.3 101.7 %reduce-scatter.13.cloned.1.call-done = f32[64,64]{1,0:T(8,128)} async-done(((f32[2048,64]{1,0:T(8,128)}), f32[64,64]{1,0:T(8,128)}) %reduce-scatter.13.cloned.1.call-update) | async-done | bytes 16400
  153.1 0.8 copy.52
  154.0 43.8 %all_gather.13 = bf16[64,2048]{0,1:T(8,128)(2,1)S(1)} all-gather(bf16[64,64]{0,1:T(8,128)(2,1)S(1)} %copy.31), channel_id=1, replica_groups=mesh['row'=16,'col'=32] {'col'}, dimensions={1}, use_global_device_ids=true | all-gather | bytes 270336 | tf_op jit(solution)/shard_map/all_gather | solution.py:52
  198.6 3.1 fusion.4
  201.7 2.4 fusion.12
  204.1 1.0 copy.59
  205.1 67.3 %reduce-scatter.9.cloned.1.call-done = f32[64,128]{1,0:T(8,128)} async-done(((f32[64,2048]{1,0:T(8,128)}), f32[64,128]{1,0:T(8,128)}) %reduce-scatter.9.cloned.1.call-update) | async-done | bytes 32784 | tf_op jit(solution)/shard_map/reduce_scatter | solution.py:60
  272.4 1.0 fusion.51
  273.4 98.9 %psum.14 = f32[64,64]{0,1:T(8,128)S(1)} all-reduce(f32[64,64]{0,1:T(8,128)S(1)} %fusion.51), channel_id=1, replica_groups=mesh['row'=16,'col'=32] {'row','col'}, use_global_device_ids=true, to_apply=%region_2.4 | all-reduce | flops 4096 | bytes 32768 | tf_op jit(solution)/shard_map/psum | solution.py:70
  372.5 5.8 cholesky.44
  379.6 4.9 custom-call.6
  384.5 1.0 fusion.22
  385.6 29.2 %all_gather.14 = bf16[64,2048]{1,0:T(8,128)(2,1)S(1)} all-gather(bf16[64,128]{1,0:T(8,128)(2,1)S(1)} %fusion.22), channel_id=1, replica_groups=mesh['row'=16,'col'=32] {'row'}, dimensions={1}, use_global_device_ids=true | all-gather | bytes 278528 | tf_op jit(solution)/shard_map/all_gather | solution.py:42
  415.4 3.6 fusion.2
  419.0 2.4 fusion.19
  421.4 1.4 copy.56
  422.8 95.3 %reduce-scatter.15.cloned.1.call-done = f32[64,64]{1,0:T(8,128)} async-done(((f32[2048,64]{1,0:T(8,128)}), f32[64,64]{1,0:T(8,128)}) %reduce-scatter.15.cloned.1.call-update) | async-done | bytes 16400
  518.1 0.8 copy.54
  519.0 43.8 %all_gather.15 = bf16[64,2048]{0,1:T(8,128)(2,1)S(1)} all-gather(bf16[64,64]{0,1:T(8,128)(2,1)S(1)} %copy.39), channel_id=1, replica_groups=mesh['row'=16,'col'=32] {'col'}, dimensions={1}, use_global_device_ids=true | all-gather | bytes 270336 | tf_op jit(solution)/shard_map/all_gather | solution.py:52
  563.6 3.1 fusion
  566.7 2.4 fusion.8
  569.1 1.0 copy.60
  570.1 67.3 %reduce-scatter.11.cloned.1.call-done = f32[64,128]{1,0:T(8,128)} async-done(((f32[64,2048]{1,0:T(8,128)}), f32[64,128]{1,0:T(8,128)}) %reduce-scatter.11.cloned.1.call-update) | async-done | bytes 32784 | tf_op jit(solution)/shard_map/reduce_scatter | solution.py:60
  637.4 1.0 fusion.48
  638.4 99.0 %psum.15 = f32[64,64]{0,1:T(8,128)S(1)} all-reduce(f32[64,64]{0,1:T(8,128)S(1)} %fusion.48), channel_id=1, replica_groups=mesh['row'=16,'col'=32] {'row','col'}, use_global_device_ids=true, to_apply=%region_7.11 | all-reduce | flops 4096 | bytes 32768 | tf_op jit(solution)/shard_map/psum | solution.py:70
  737.5 5.8 cholesky.55
  744.7 4.9 custom-call.7
  749.6 1.6 convolution_multiply_fusion
  (38 shorter events, 9.9 us)
Async XLA Ops:
  6.5 146.5 %reduce-scatter.13.cloned.1.call-start = ((), (), s32[]{:S(2)}) async-start(), calls=%async_computation.6 | async-start | bytes 1081344
  50.5 221.9 %reduce-scatter.9.cloned.1.call-start = ((), (), s32[]{:S(2)}) async-start(), calls=%async_computation.4 | async-start | bytes 557056 | tf_op jit(solution)/shard_map/reduce_scatter | solution.py:60
  205.0 313.1 %reduce-scatter.15.cloned.1.call-start = ((), (), s32[]{:S(2)}) async-start(), calls=%async_computation.7 | async-start | bytes 1081344
  422.8 214.6 %reduce-scatter.11.cloned.1.call-start = ((), (), s32[]{:S(2)}) async-start(), calls=%async_computation.5 | async-start | bytes 557056 | tf_op jit(solution)/shard_map/reduce_scatter | solution.py:60
Sparse Core Ops, SparseCore 0:
  50.6 102.3 reduce-scatter.12
  205.2 67.2 reduce-scatter.8
  422.9 95.1 reduce-scatter.14
  570.2 67.1 reduce-scatter.10
where the time goes:
time: 759 us; the launch traced here: 758 us
  blocking collectives  347 us (46%)
  waiting for transfers between devices  332 us (44%)
  matrix products  27.4 us (4%)
  other arithmetic  27.3 us (4%)
  between operations  14 us (2%)
  local copies, waits for them, and re-layouts  10.3 us (1%)
    psum x2, blocking collectives, shards(): lax.psum(jnp.einsum('ri,si->rs', lifted, lifted, precision=HIGH), ('row',...  198 us
    unnamed x6, waiting for transfers between devices  197 us
    reduce_scatter x2, waiting for transfers between devices, shards(): lax.psum_scatter(jnp.einsum('kp,krj->rpj', col_hot, backward_products, pr...  135 us
    all_gather x2, blocking collectives, shards(): query_block = lax.all_gather(rounded, 'col', axis=1, tiled=True)  87.6 us
    all_gather x2, blocking collectives, shards(): scaled_block = lax.all_gather(scaled, 'row', axis=1, tiled=True)  61.5 us
  transfers between devices with their start and end apart: 4, of which 4 were waited for; matrix products, arithmetic and copies ran while one was open for 0% of the time, Pallas kernels for 0%

commit v1 on v0

--- a/solution.py
+++ b/solution.py
@@ -39,7 +39,9 @@
     current = panel
     for iteration in range(ITERS):
         scaled = (current * my_pscale[None, :]).astype(jnp.bfloat16)
-        scaled_block = lax.all_gather(scaled, "row", axis=1, tiled=True)
+        scaled_block = jnp.concatenate(
+            lax.all_to_all(jnp.stack([scaled] * lax.axis_size("row")), "row", 0, 0), axis=1
+        )
         picked = jnp.take(scaled_block.reshape(width, product_tiles, side), slot_ids[1], axis=1)
         products = jnp.einsum("rkj,kij->kri", picked, tile_set, preferred_element_type=jnp.float32)
         partial_sum = jnp.einsum("kq,kri->rqi", row_hot, products, precision=HIGH).reshape(

time: 759 us -> 724 us (0.954)
  blocking collectives: 347 us -> 301 us
  starting transfers between devices: 0.13 us -> 9.31 us
    all_gather x2 -> x0, blocking collectives: 61.5 us -> none  [shards(): scaled_block = lax.all_gather(scaled, 'row', axis=1, tiled=True)]
    all_to_all x0 -> x1, blocking collectives: none -> 15.3 us  [shards(): lax.all_to_all(jnp.stack([scaled] * lax.axis_size('row')), 'row', 0, 0)]
    all_to_all x0 -> x1, starting transfers between devices: none -> 9.15 us  [shards(): lax.all_to_all(jnp.stack([scaled] * lax.axis_size('row')), 'row', 0, 0)]
  transfers between devices with their start and end apart: 4 -> 5, of which waited for: 4 -> 5; matrix products, arithmetic and copies ran while one was open for 0% -> 0% of each run, Pallas kernels for 0% -> 0%
where the time goes in v1:
time: 724 us; the launch traced here: 723 us
  waiting for transfers between devices  333 us (46%)
  blocking collectives  301 us (42%)
  matrix products  27.4 us (4%)
  other arithmetic  27.2 us (4%)
  between operations  14 us (2%)
  local copies, waits for them, and re-layouts  11.6 us (2%)
  starting transfers between devices  9.31 us (1%)
    psum x2, blocking collectives, shards(): lax.psum(jnp.einsum('ri,si->rs', lifted, lifted, precision=HIGH), ('row',...  198 us
    unnamed x6, waiting for transfers between devices  190 us
    reduce_scatter x2, waiting for transfers between devices, shards(): lax.psum_scatter(jnp.einsum('kp,krj->rpj', col_hot, backward_products, pr...  135 us
    all_gather x2, blocking collectives, shards(): query_block = lax.all_gather(rounded, 'col', axis=1, tiled=True)  87.7 us
    all_to_all x1, blocking collectives, shards(): lax.all_to_all(jnp.stack([scaled] * lax.axis_size('row')), 'row', 0, 0)  15.3 us
  transfers between devices with their start and end apart: 5, of which 5 were waited for; matrix products, arithmetic and copies ran while one was open for 0% of the time, Pallas kernels for 0%

profile of v1, /device:TPU:24, one launch (start us, length us, event | category | flops | bytes accessed | tf_op | source)
XLA Modules:
  0.0 723.2 jit_solution(14288274045298849954)
XLA Ops:
  8.8 9.1 %all-to-all-start = ((bf16[16,64,128]{2,1,0:T(8,128)(2,1)}), bf16[16,64,128]{2,1,0:T(8,128)(2,1)S(1)}, u32[]{:S(2)}, u32[]{:S(2)}) async-start(bf16[16,64,128]{2,1,0:T(8,128)(2,1)} %stack.4), calls=%async_computation | async-start | bytes 524288 | tf_op jit(solution)/shard_map/all_to_all | solution.py:43
  20.2 7.3 %all-to-all-done = bf16[16,64,128]{2,1,0:T(8,128)(2,1)S(1)} async-done(((bf16[16,64,128]{2,1,0:T(8,128)(2,1)}), bf16[16,64,128]{2,1,0:T(8,128)(2,1)S(1)}, u32[]{:S(2)}, u32[]{:S(2)}) %all-to-all-start) | async-done | bytes 262176 | tf_op jit(solution)/shard_map/all_to_all | solution.py:43
  28.4 3.6 fusion.6
  32.0 2.4 fusion.16
  34.4 1.4 copy.57
  36.6 98.5 %reduce-scatter.13.cloned.1.call-done = f32[64,64]{1,0:T(8,128)} async-done(((f32[2048,64]{1,0:T(8,128)}), f32[64,64]{1,0:T(8,128)}) %reduce-scatter.13.cloned.1.call-update) | async-done | bytes 16400
  135.0 0.8 copy.54
  136.0 43.8 %all_gather.6 = bf16[64,2048]{0,1:T(8,128)(2,1)S(1)} all-gather(bf16[64,64]{0,1:T(8,128)(2,1)S(1)} %copy.32), channel_id=1, replica_groups=mesh['row'=16,'col'=32] {'col'}, dimensions={1}, use_global_device_ids=true | all-gather | bytes 270336 | tf_op jit(solution)/shard_map/all_gather | solution.py:54
  180.6 3.1 fusion.4
  183.7 2.4 fusion.12
  186.1 1.0 copy.59
  187.1 67.5 %reduce-scatter.9.cloned.1.call-done = f32[64,128]{1,0:T(8,128)} async-done(((f32[64,2048]{1,0:T(8,128)}), f32[64,128]{1,0:T(8,128)}) %reduce-scatter.9.cloned.1.call-update) | async-done | bytes 32784 | tf_op jit(solution)/shard_map/reduce_scatter | solution.py:62
  254.6 1.0 fusion.51
  255.6 99.0 %psum.14 = f32[64,64]{0,1:T(8,128)S(1)} all-reduce(f32[64,64]{0,1:T(8,128)S(1)} %fusion.51), channel_id=1, replica_groups=mesh['row'=16,'col'=32] {'row','col'}, use_global_device_ids=true, to_apply=%region_2.4 | all-reduce | flops 4096 | bytes 32768 | tf_op jit(solution)/shard_map/psum | solution.py:72
  354.7 5.8 cholesky.44
  361.9 4.9 custom-call.6
  366.8 1.0 fusion.22
  367.9 15.3 %all_to_all.10 = bf16[16,64,128]{2,1,0:T(8,128)(2,1)S(1)} all-to-all(bf16[16,64,128]{2,1,0:T(8,128)(2,1)S(1)} %stack.5), channel_id=1, replica_groups=mesh['row'=16,'col'=32] {'row'}, dimensions={0} | all-to-all | bytes 524288 | tf_op jit(solution)/shard_map/all_to_all | solution.py:43
  384.2 3.6 fusion.2
  387.8 2.4 fusion.19
  390.1 1.4 copy.58
  391.6 91.9 %reduce-scatter.15.cloned.1.call-done = f32[64,64]{1,0:T(8,128)} async-done(((f32[2048,64]{1,0:T(8,128)}), f32[64,64]{1,0:T(8,128)}) %reduce-scatter.15.cloned.1.call-update) | async-done | bytes 16400
  484.4 43.8 %all_gather.7 = bf16[64,2048]{0,1:T(8,128)(2,1)S(1)} all-gather(bf16[64,64]{0,1:T(8,128)(2,1)S(1)} %copy.41), channel_id=1, replica_groups=mesh['row'=16,'col'=32] {'col'}, dimensions={1}, use_global_device_ids=true | all-gather | bytes 270336 | tf_op jit(solution)/shard_map/all_gather | solution.py:54
  529.0 3.1 fusion
  532.1 2.4 fusion.8
  534.5 1.0 copy.60
  535.4 67.3 %reduce-scatter.11.cloned.1.call-done = f32[64,128]{1,0:T(8,128)} async-done(((f32[64,2048]{1,0:T(8,128)}), f32[64,128]{1,0:T(8,128)}) %reduce-scatter.11.cloned.1.call-update) | async-done | bytes 32784 | tf_op jit(solution)/shard_map/reduce_scatter | solution.py:62
  602.8 1.0 fusion.48
  603.8 99.1 %psum.15 = f32[64,64]{0,1:T(8,128)S(1)} all-reduce(f32[64,64]{0,1:T(8,128)S(1)} %fusion.48), channel_id=1, replica_groups=mesh['row'=16,'col'=32] {'row','col'}, use_global_device_ids=true, to_apply=%region_7.11 | all-reduce | flops 4096 | bytes 32768 | tf_op jit(solution)/shard_map/psum | solution.py:72
  703.0 5.8 cholesky.55
  710.2 4.9 custom-call.7
  715.0 1.6 convolution_multiply_fusion
  (45 shorter events, 12.2 us)
Async XLA Ops:
  8.8 18.7 %all-to-all-start = ((bf16[16,64,128]{2,1,0:T(8,128)(2,1)}), bf16[16,64,128]{2,1,0:T(8,128)(2,1)S(1)}, u32[]{:S(2)}, u32[]{:S(2)}) async-start(bf16[16,64,128]{2,1,0:T(8,128)(2,1)} %stack.4), calls=%async_computation | async-start | bytes 524288 | tf_op jit(solution)/shard_map/all_to_all | solution.py:43
  18.0 117.1 %reduce-scatter.13.cloned.1.call-start = ((), (), s32[]{:S(2)}) async-start(), calls=%async_computation.8 | async-start | bytes 1081344
  35.8 218.8 %reduce-scatter.9.cloned.1.call-start = ((), (), s32[]{:S(2)}) async-start(), calls=%async_computation.6 | async-start | bytes 557056 | tf_op jit(solution)/shard_map/reduce_scatter | solution.py:62
  187.0 296.4 %reduce-scatter.15.cloned.1.call-start = ((), (), s32[]{:S(2)}) async-start(), calls=%async_computation.9 | async-start | bytes 1081344
  391.5 211.3 %reduce-scatter.11.cloned.1.call-start = ((), (), s32[]{:S(2)}) async-start(), calls=%async_computation.7 | async-start | bytes 557056 | tf_op jit(solution)/shard_map/reduce_scatter | solution.py:62
Sparse Core Ops, SparseCore 0:
  35.9 99.1 reduce-scatter.12
  187.2 67.3 reduce-scatter.8
  391.6 91.7 reduce-scatter.14
  535.6 67.1 reduce-scatter.10
